TPU v7x, 32 devices: a whole 2x2x4 slice. The times are simulated.
32 devices in a mesh: dp: 8 (over z, x), th: 2 (over core), tw: 2 (over y).
Axes of the slice: x: 2, y: 2, z: 4, core: 2. Of those that a mesh axis runs over, the one named last changes fastest.
Arguments:
- tokens: bfloat16 [16, 1536, 768], P('dp', ('th', 'tw')), may hold values from -6 to 6
- segment_ids: int32 [16, 1536], P('dp'), may hold values from 0 to 7, never falling along the last dimension, each value on 1 to 768 neighbouring positions
- norm1_gain: float32 [768], replicated, may hold values from 0.5 to 1.5
- norm1_shift: float32 [768], replicated, may hold values from -3 to 3
- w_qkv: bfloat16 [3, 768, 768], P(None, None, ('th', 'tw')), may hold values from -0.21875 to 0.21875
- b_qv: float32 [2, 768], P(None, ('th', 'tw')), may hold values from -3 to 3
- w_out: bfloat16 [768, 768], P(('th', 'tw')), may hold values from -0.875 to 0.875
- b_out: float32 [768], replicated, may hold values from -3 to 3
- norm2_gain: float32 [768], replicated, may hold values from 0.5 to 1.5
- norm2_shift: float32 [768], replicated, may hold values from -3 to 3
- w_up: bfloat16 [768, 3072], replicated, may hold values from -0.21875 to 0.21875
- b_up: float32 [3072], replicated, may hold values from -3 to 3
- w_down: bfloat16 [3072, 768], replicated, may hold values from -0.109375 to 0.109375
- b_down: float32 [768], replicated, may hold values from -3 to 3
- cotangent: bfloat16 [16, 1536, 768], P('dp', ('th', 'tw')), may hold values from -6 to 6
Outputs:
- block_out: bfloat16 [16, 1536, 768], P('dp', ('th', 'tw'))
- grad_tokens: bfloat16 [16, 1536, 768], P('dp', ('th', 'tw'))
- grad_norm1_gain: float32 [768], replicated
- grad_norm1_shift: float32 [768], replicated
- grad_w_qkv: float32 [3, 768, 768], P(None, None, ('th', 'tw'))
- grad_b_qv: float32 [2, 768], P(None, ('th', 'tw'))
- grad_w_out: float32 [768, 768], P(('th', 'tw'))
- grad_b_out: float32 [768], replicated
- grad_norm2_gain: float32 [768], replicated
- grad_norm2_shift: float32 [768], replicated
- grad_w_up: float32 [768, 3072], replicated
- grad_b_up: float32 [3072], replicated
- grad_w_down: float32 [3072, 768], replicated
- grad_b_down: float32 [768], replicated
Inputs may be any that keep to these rules, and one draw needn't show every extreme that they name: `segment_ids`: within each row the ids never fall, and one image holds 1 to 768 tokens.
All inputs are finite; a program needn't handle non-finite values.
Results may differ from a plain program's by a relative error of at most 0.015.
Values may be sent and summed in bfloat16 or wider, within the bound.
A program may use at most 192 MiB of HBM per device.

v0:
```python
import jax
import jax.numpy as jnp
from jax import lax
from jax.sharding import PartitionSpec as P

HD = 64
EPSILON = 1e-06


def layer_norm(field, norm_gain, norm_shift):
    average = jnp.mean(field, axis=-1, keepdims=True)
    centred = field - average
    spread = jnp.mean(centred * centred, axis=-1, keepdims=True)
    return centred * lax.rsqrt(spread + EPSILON) * norm_gain + norm_shift


def gelu_exact(field):
    return jax.nn.gelu(field, approximate=False)


def masked_scores(query_block, key_rows, row_seg, offset, block_rows):
    score_scale = query_block.shape[-1] ** (-0.5)
    same_image = row_seg[offset : offset + block_rows, None] == row_seg[None, :]
    scores = (
        jnp.einsum("qhe,khe->hqk", query_block, key_rows, preferred_element_type=jnp.float32)
        * score_scale
    )
    return jnp.where(same_image[None], scores, -1000000000.0)


def row_forward(row_items):
    row_qkv, row_seg = row_items
    length = row_qkv.shape[1]
    head_count = row_qkv.shape[2] // HD
    key_rows = row_qkv[1].reshape(length, head_count, HD)
    value_rows = row_qkv[2].reshape(length, head_count, HD)
    block_rows = min(512, length)
    head_outs = []
    log_totals = []
    for offset in range(0, length, block_rows):
        query_block = row_qkv[0, offset : offset + block_rows].reshape(block_rows, head_count, HD)
        scores = masked_scores(query_block, key_rows, row_seg, offset, block_rows)
        row_peak = jnp.max(scores, axis=-1, keepdims=True)
        exponent = jnp.exp(scores - row_peak)
        denominator = jnp.sum(exponent, axis=-1, keepdims=True)
        weights_low = (exponent / denominator).astype(jnp.bfloat16)
        head_out = jnp.einsum(
            "hqk,khe->qhe", weights_low, value_rows, preferred_element_type=jnp.float32
        )
        head_outs.append(head_out.reshape(block_rows, head_count * HD).astype(jnp.bfloat16))
        log_totals.append((row_peak + jnp.log(denominator))[..., 0])
    return (jnp.concatenate(head_outs, 0), jnp.concatenate(log_totals, 1))


def row_backward(row_items):
    row_qkv, row_grad, row_total, row_seg = row_items
    length = row_qkv.shape[1]
    head_count = row_qkv.shape[2] // HD
    score_scale = HD ** (-0.5)
    key_rows = row_qkv[1].reshape(length, head_count, HD)
    value_rows = row_qkv[2].reshape(length, head_count, HD)
    block_rows = min(512, length)
    key_grad = jnp.zeros((length, head_count, HD), jnp.float32)
    value_grad = jnp.zeros((length, head_count, HD), jnp.float32)
    query_grads = []
    for offset in range(0, length, block_rows):
        query_block = row_qkv[0, offset : offset + block_rows].reshape(block_rows, head_count, HD)
        upstream = row_grad[offset : offset + block_rows].reshape(block_rows, head_count, HD)
        scores = masked_scores(query_block, key_rows, row_seg, offset, block_rows)
        probability = jnp.exp(scores - row_total[:, offset : offset + block_rows, None])
        value_grad = value_grad + jnp.einsum(
            "hqk,qhe->khe",
            probability.astype(jnp.bfloat16),
            upstream,
            preferred_element_type=jnp.float32,
        )
        prob_grad = jnp.einsum(
            "qhe,khe->hqk", upstream, value_rows, preferred_element_type=jnp.float32
        )
        row_inner = jnp.sum(probability * prob_grad, axis=-1, keepdims=True)
        score_grad = (probability * (prob_grad - row_inner)).astype(jnp.bfloat16) * score_scale
        query_grad = jnp.einsum(
            "hqk,khe->qhe", score_grad, key_rows, preferred_element_type=jnp.float32
        )
        query_grads.append(query_grad.reshape(block_rows, head_count * HD))
        key_grad = key_grad + jnp.einsum(
            "hqk,qhe->khe", score_grad, query_block, preferred_element_type=jnp.float32
        )
    stacked = jnp.stack(
        [
            jnp.concatenate(query_grads, 0),
            key_grad.reshape(length, head_count * HD),
            value_grad.reshape(length, head_count * HD),
        ]
    )
    return stacked.astype(jnp.bfloat16)


def body(
    tokens,
    segment_ids,
    norm1_gain,
    norm1_shift,
    w_qkv,
    b_qv,
    w_out,
    b_out,
    norm2_gain,
    norm2_shift,
    w_up,
    b_up,
    w_down,
    b_down,
    cotangent,
):
    inputs = tokens.astype(jnp.float32)
    normed_one, norm_one_back = jax.vjp(layer_norm, inputs, norm1_gain, norm1_shift)
    normed_low = normed_one.astype(jnp.bfloat16)
    gathered = lax.all_gather(normed_low, ("th", "tw"), axis=1, tiled=True)
    bias_rows = jnp.stack([b_qv[0], jnp.zeros_like(b_qv[0]), b_qv[1]])
    projected = jnp.einsum("rld,cde->rcle", gathered, w_qkv, preferred_element_type=jnp.float32)
    projected_low = (projected + bias_rows[None, :, None, :]).astype(jnp.bfloat16)
    heads_out, totals = lax.map(row_forward, (projected_low, segment_ids))
    partial_out = jnp.einsum("rle,ed->rld", heads_out, w_out, preferred_element_type=jnp.float32)
    branch = (
        lax.psum_scatter(
            partial_out.astype(jnp.bfloat16), ("th", "tw"), scatter_dimension=1, tiled=True
        ).astype(jnp.float32)
        + b_out
    )
    middle = inputs + branch
    normed_two, norm_two_back = jax.vjp(layer_norm, middle, norm2_gain, norm2_shift)
    second_low = normed_two.astype(jnp.bfloat16)
    hidden_pre = (
        jnp.einsum("rld,df->rlf", second_low, w_up, preferred_element_type=jnp.float32) + b_up
    )
    activated, gelu_back = jax.vjp(gelu_exact, hidden_pre)
    active_low = activated.astype(jnp.bfloat16)
    block_out = middle + (
        jnp.einsum("rlf,fd->rld", active_low, w_down, preferred_element_type=jnp.float32) + b_down
    )
    upstream = cotangent.astype(jnp.float32)
    grad_w_down = jnp.einsum(
        "rlf,rld->fd", active_low, cotangent, preferred_element_type=jnp.float32
    )
    grad_b_down = jnp.sum(upstream, axis=(0, 1))
    grad_active = jnp.einsum("rld,fd->rlf", cotangent, w_down, preferred_element_type=jnp.float32)
    grad_hidden = gelu_back(grad_active)[0].astype(jnp.bfloat16)
    grad_w_up = jnp.einsum(
        "rld,rlf->df", second_low, grad_hidden, preferred_element_type=jnp.float32
    )
    grad_b_up = jnp.sum(grad_hidden.astype(jnp.float32), axis=(0, 1))
    grad_normed_two = jnp.einsum(
        "rlf,df->rld", grad_hidden, w_up, preferred_element_type=jnp.float32
    )
    grad_mid_norm, grad_gain_two, grad_shift_two = norm_two_back(grad_normed_two)
    grad_middle = upstream + grad_mid_norm
    grad_branch = grad_middle.astype(jnp.bfloat16)
    grad_b_out = jnp.sum(grad_branch.astype(jnp.float32), axis=(0, 1))
    grad_whole = lax.all_gather(grad_branch, ("th", "tw"), axis=1, tiled=True)
    grad_heads = jnp.einsum(
        "rld,ed->rle", grad_whole, w_out, preferred_element_type=jnp.float32
    ).astype(jnp.bfloat16)
    grad_w_out = jnp.einsum(
        "rle,rld->ed", heads_out, grad_whole, preferred_element_type=jnp.float32
    )
    grad_qkv = lax.map(row_backward, (projected_low, grad_heads, totals, segment_ids))
    grad_w_qkv = jnp.einsum("rld,rcle->cde", gathered, grad_qkv, preferred_element_type=jnp.float32)
    grad_b_qv = jnp.sum(grad_qkv[:, 0::2].astype(jnp.float32), axis=(0, 2))
    grad_normed = jnp.einsum("rcle,cde->rld", grad_qkv, w_qkv, preferred_element_type=jnp.float32)
    grad_tile = lax.psum_scatter(
        grad_normed.astype(jnp.bfloat16), ("th", "tw"), scatter_dimension=1, tiled=True
    ).astype(jnp.float32)
    grad_inputs, grad_gain_one, grad_shift_one = norm_one_back(grad_tile)
    grad_tokens = (grad_middle + grad_inputs).astype(jnp.bfloat16)
    head_sums = (
        lax.psum(grad_w_qkv.astype(jnp.bfloat16), "dp").astype(jnp.float32),
        lax.psum(grad_b_qv.astype(jnp.bfloat16), "dp").astype(jnp.float32),
        lax.psum(grad_w_out.astype(jnp.bfloat16), "dp").astype(jnp.float32),
    )
    shared = lax.psum(
        (
            grad_gain_one,
            grad_shift_one,
            grad_b_out,
            grad_gain_two,
            grad_shift_two,
            grad_w_up,
            grad_b_up,
            grad_w_down,
            grad_b_down,
        ),
        ("dp", "th", "tw"),
    )
    return (
        block_out.astype(jnp.bfloat16),
        grad_tokens,
        shared[0],
        shared[1],
        head_sums[0],
        head_sums[1],
        head_sums[2],
        shared[2],
        shared[3],
        shared[4],
        shared[5],
        shared[6],
        shared[7],
        shared[8],
    )


def solution(mesh):
    return jax.shard_map(
        body,
        mesh=mesh,
        in_specs=(
            P("dp", ("th", "tw"), None),
            P("dp", None),
            P(),
            P(),
            P(None, None, ("th", "tw")),
            P(None, ("th", "tw")),
            P(("th", "tw"), None),
            P(),
            P(),
            P(),
            P(),
            P(),
            P(),
            P(),
            P("dp", ("th", "tw"), None),
        ),
        out_specs=(
            P("dp", ("th", "tw"), None),
            P("dp", ("th", "tw"), None),
            P(),
            P(),
            P(None, None, ("th", "tw")),
            P(None, ("th", "tw")),
            P(("th", "tw"), None),
            P(),
            P(),
            P(),
            P(),
            P(),
            P(),
            P(),
        ),
        check_vma=False,
    )
```

profile of v0, /device:TPU:0, one launch (start us, length us, event | category | flops | bytes accessed | tf_op | source)
XLA Modules:
  0.0 1006.1 jit_solution(13144696597506998621)
XLA Ops:
  11.7 2.8 fusion.160
  14.8 40.1 %all-gather.3.cloned.1.call-done = bf16[2,1536,768]{2,1,0:T(8,128)(2,1)} async-done(((bf16[2,384,768]{2,1,0:T(8,128)(2,1)}), bf16[2,1536,768]{2,1,0:T(8,128)(2,1)}) %all-gather.3.cloned.1.call-update) | async-done | bytes 4718608 | tf_op jit(solution)/shard_map/all_gather | solution.py:119
  54.9 6.7 fusion.154
  61.6 59.3 %while.22 = (s32[]{:T(128)}, bf16[2,1536,192]{1,2,0:T(8,128)(2,1)S(1)}, f32[2,3,1536]{2,1,0:T(4,128)S(1)}, bf16[2,3,1536,192]{2,3,1,0:T(8,128)(2,1)}, s32[2,1536...) while((s32[]{:T(128)}, bf16[2,1536,192]{1,2,0:T(8,128)(2,1)S(1)}, ...), condition=%wide.region_9.10_spmd, body=%wide.region_2.9_spmd.sunk | while | flops 1901302272 | bytes 107581632 | solution.py:123
  68.4 2.8 fusion.320
  71.2 3.5 fusion.321
  78.7 5.2 fusion.324
  83.9 3.5 fusion.326
  87.4 3.5 fusion.325
  97.6 2.8 fusion.320
  100.4 3.5 fusion.321
  108.0 5.2 fusion.324
  113.1 3.5 fusion.326
  116.7 3.5 fusion.325
  120.9 4.9 convolution_convert_fusion
  125.9 47.9 %reduce-scatter.3.cloned.1.call-done = bf16[2,384,768]{2,1,0:T(8,128)(2,1)} async-done(((bf16[2,1536,768]{2,1,0:T(8,128)(2,1)}), bf16[2,384,768]{2,1,0:T(8,128)(2,1)}) %reduce-scatter.3.cloned.1.call-update) | async-done | bytes 1179664 | tf_op jit(solution)/shard_map/reduce_scatter | solution.py:126
  177.7 9.2 fusion.165
  186.9 23.4 %multiply_convert_fusion.3 = (bf16[2,384,3072]{2,1,0:T(8,128)(2,1)}, f32[2,384,3072]{2,1,0:T(8,128)}) fusion(f32[2,384,3072]{2,1,0:T(8,128)S(1)} %get-tuple-element.164, f32[3072]{0:T(1024)S(1)} %copy-done.45, u8[384,3072]{1,0:T(8,128)(4,1)S(1)} %get-tuple-element.78, u8[384,3072]{1,0:T(8,128)(4,1)S(1)} %get-tuple-element.77), kind=kLoop, calls=%fused_computation.126 | loop fusion | flops 167510016 | bytes 25964544 | tf_op jit(solution)/shard_map/convert_element_type | solution.py:138
  210.2 12.5 %convert_reduce_fusion = (f32[3072]{0:T(1024)}, bf16[2,384,3072]{2,1,0:T(8,128)(2,1)}) fusion(f32[2,384,3072]{2,1,0:T(8,128)} %get-tuple-element.123, bf16[2,384,768]{2,1,0:T(8,128)(2,1)S(1)} %copy-done.15, bf16[3072,768]{1,0:T(8,128)(2,1)} %param.31, f32[2,384,3072]{2,1,0:T(8,128)S(1)} %get-tuple-element.164, f32[3072]{0:T(1024)S(1)} %copy-done.45), kind=kOutput, calls=%fused_computation.124 | convolution fusion | flops 3663983616 | bytes 29515776 | tf_op jit(solution)/shard_map/rld,fd->rlf/dot_general | solution.py:147
  222.8 8.1 fusion.185
  232.9 2.7 convert_reduce_fusion.4
  235.7 37.6 %all-gather.5.cloned.1.call-done = bf16[2,1536,768]{2,1,0:T(8,128)(2,1)} async-done(((bf16[2,384,768]{2,1,0:T(8,128)(2,1)}), bf16[2,1536,768]{2,1,0:T(8,128)(2,1)}) %all-gather.5.cloned.1.call-update) | async-done | bytes 4718608 | tf_op jit(solution)/shard_map/all_gather | solution.py:160
  273.3 5.0 convolution_convert_fusion.1
  278.3 254.2 %while.23 = (s32[]{:T(128)}, bf16[2,3,1536,192]{2,3,1,0:T(8,128)(2,1)}, bf16[2,3,1536,192]{2,3,1,0:T(8,128)(2,1)}, s32[2,1536]{1,0:T(2,128)S(1)}, f32[2,3,1536]{...) while((s32[]{:T(128)}, ...), condition=%wide.region_19.20_spmd, body=%wide.region_15.19_spmd.sunk | while | flops 4682926080 | bytes 364640672 | solution.py:167
  283.2 2.5 subtract_exponential_fusion.9
  286.7 2.6 copy-done.2
  289.3 2.5 subtract_exponential_fusion.11
  294.2 4.3 copy-done.3
  300.4 5.2 fusion.371
  305.6 15.2 %fusion.377 = bf16[3,64,512]{2,1,0:T(8,128)(2,1)} fusion(bf16[1536,3,64]{0,2,1:T(8,128)(2,1)S(1)} %bitcast.312, f32[3,512,1536]{2,1,0:T(8,128)} %copy-done.4, f32[3,512,1536]{2,1,0:T(8,128)} %fusion.371), kind=kOutput, calls=%fused_computation.94.clone.1 | convolution fusion | flops 320965632 | bytes 19660800 | tf_op jit(solution)/shard_map/while/body/eval_jaxpr/hqk,khe->qhe/dot_general | solution.py:82
  320.8 15.3 %fusion.372 = f32[3,64,1536]{2,1,0:T(8,128)} fusion(bf16[512,3,64]{0,2,1:T(8,128)(2,1)} %bitcast.323, f32[3,512,1536]{2,1,0:T(8,128)} %copy-done.4, f32[3,512,1536]{2,1,0:T(8,128)} %fusion.371), kind=kOutput, calls=%fused_computation.63.clone.1 | convolution fusion | flops 320867328 | bytes 20250624 | tf_op jit(solution)/shard_map/while/body/eval_jaxpr/hqk,qhe->khe/dot_general | solution.py:86
  336.1 5.2 fusion.375
  341.3 14.4 %fusion.379 = bf16[3,64,512]{2,1,0:T(8,128)(2,1)S(1)} fusion(bf16[1536,3,64]{0,2,1:T(8,128)(2,1)S(1)} %bitcast.313, f32[3,512,1536]{2,1,0:T(8,128)} %copy-done.3, f32[3,512,1536]{2,1,0:T(8,128)} %fusion.375), kind=kOutput, calls=%fused_computation.92.clone.1 | convolution fusion | flops 320965632 | bytes 19660800 | tf_op jit(solution)/shard_map/while/body/eval_jaxpr/hqk,khe->qhe/dot_general | solution.py:82
  355.6 5.2 fusion.373
  360.8 15.0 %fusion.378 = bf16[3,64,512]{2,1,0:T(8,128)(2,1)} fusion(bf16[1536,3,64]{0,2,1:T(8,128)(2,1)S(1)} %bitcast.314, f32[3,512,1536]{2,1,0:T(8,128)} %copy-done.2, f32[3,512,1536]{2,1,0:T(8,128)} %fusion.373), kind=kOutput, calls=%fused_computation.93.clone.1 | convolution fusion | flops 320965632 | bytes 19660800 | tf_op jit(solution)/shard_map/while/body/eval_jaxpr/hqk,khe->qhe/dot_general | solution.py:82
  375.8 14.1 %fusion.374 = f32[3,64,1536]{2,1,0:T(8,128)} fusion(bf16[512,3,64]{0,2,1:T(8,128)(2,1)S(1)} %bitcast.321, f32[3,512,1536]{2,1,0:T(8,128)} %copy-done.2, f32[3,512,1536]{2,1,0:T(8,128)} %fusion.373), kind=kOutput, calls=%fused_computation.67.clone.1 | convolution fusion | flops 320867328 | bytes 20250624 | tf_op jit(solution)/shard_map/while/body/eval_jaxpr/hqk,qhe->khe/dot_general | solution.py:86
  389.9 14.1 %fusion.376 = bf16[3,64,1536]{2,1,0:T(8,128)(2,1)S(1)} fusion(f32[3,64,1536]{2,1,0:T(8,128)} %fusion.372, f32[3,64,1536]{2,1,0:T(8,128)} %fusion.374, bf16[512,3,64]{0,2,1:T(8,128)(2,1)S(1)} %bitcast.319, f32[3,512,1536]{2,1,0:T(8,128)} %copy-done.3, f32[3,512,1536]{2,1,0:T(8,128)} %fusion.375), kind=kOutput, calls=%fused_computation.79.clone.1 | convolution fusion | flops 321752064 | bytes 22020096 | tf_op jit(solution)/shard_map/while/body/eval_jaxpr/hqk,qhe->khe/dot_general | solution.py:86
  413.5 2.6 copy-done.2
  421.0 4.3 copy-done.3
  427.2 5.2 fusion.371
  432.4 15.2 %fusion.377 = bf16[3,64,512]{2,1,0:T(8,128)(2,1)} fusion(bf16[1536,3,64]{0,2,1:T(8,128)(2,1)S(1)} %bitcast.312, f32[3,512,1536]{2,1,0:T(8,128)} %copy-done.4, f32[3,512,1536]{2,1,0:T(8,128)} %fusion.371), kind=kOutput, calls=%fused_computation.94.clone.1 | convolution fusion | flops 320965632 | bytes 19660800 | tf_op jit(solution)/shard_map/while/body/eval_jaxpr/hqk,khe->qhe/dot_general | solution.py:82
  447.6 15.3 %fusion.372 = f32[3,64,1536]{2,1,0:T(8,128)} fusion(bf16[512,3,64]{0,2,1:T(8,128)(2,1)} %bitcast.323, f32[3,512,1536]{2,1,0:T(8,128)} %copy-done.4, f32[3,512,1536]{2,1,0:T(8,128)} %fusion.371), kind=kOutput, calls=%fused_computation.63.clone.1 | convolution fusion | flops 320867328 | bytes 20250624 | tf_op jit(solution)/shard_map/while/body/eval_jaxpr/hqk,qhe->khe/dot_general | solution.py:86
  462.9 5.2 fusion.375
  468.1 14.4 %fusion.379 = bf16[3,64,512]{2,1,0:T(8,128)(2,1)S(1)} fusion(bf16[1536,3,64]{0,2,1:T(8,128)(2,1)S(1)} %bitcast.313, f32[3,512,1536]{2,1,0:T(8,128)} %copy-done.3, f32[3,512,1536]{2,1,0:T(8,128)} %fusion.375), kind=kOutput, calls=%fused_computation.92.clone.1 | convolution fusion | flops 320965632 | bytes 19660800 | tf_op jit(solution)/shard_map/while/body/eval_jaxpr/hqk,khe->qhe/dot_general | solution.py:82
  482.5 5.2 fusion.373
  487.6 15.0 %fusion.378 = bf16[3,64,512]{2,1,0:T(8,128)(2,1)} fusion(bf16[1536,3,64]{0,2,1:T(8,128)(2,1)S(1)} %bitcast.314, f32[3,512,1536]{2,1,0:T(8,128)} %copy-done.2, f32[3,512,1536]{2,1,0:T(8,128)} %fusion.373), kind=kOutput, calls=%fused_computation.93.clone.1 | convolution fusion | flops 320965632 | bytes 19660800 | tf_op jit(solution)/shard_map/while/body/eval_jaxpr/hqk,khe->qhe/dot_general | solution.py:82
  502.6 14.1 %fusion.374 = f32[3,64,1536]{2,1,0:T(8,128)} fusion(bf16[512,3,64]{0,2,1:T(8,128)(2,1)S(1)} %bitcast.321, f32[3,512,1536]{2,1,0:T(8,128)} %copy-done.2, f32[3,512,1536]{2,1,0:T(8,128)} %fusion.373), kind=kOutput, calls=%fused_computation.67.clone.1 | convolution fusion | flops 320867328 | bytes 20250624 | tf_op jit(solution)/shard_map/while/body/eval_jaxpr/hqk,qhe->khe/dot_general | solution.py:86
  516.8 14.1 %fusion.376 = bf16[3,64,1536]{2,1,0:T(8,128)(2,1)S(1)} fusion(f32[3,64,1536]{2,1,0:T(8,128)} %fusion.372, f32[3,64,1536]{2,1,0:T(8,128)} %fusion.374, bf16[512,3,64]{0,2,1:T(8,128)(2,1)S(1)} %bitcast.319, f32[3,512,1536]{2,1,0:T(8,128)} %copy-done.3, f32[3,512,1536]{2,1,0:T(8,128)} %fusion.375), kind=kOutput, calls=%fused_computation.79.clone.1 | convolution fusion | flops 321752064 | bytes 22020096 | tf_op jit(solution)/shard_map/while/body/eval_jaxpr/hqk,qhe->khe/dot_general | solution.py:86
  532.5 4.6 fusion.177
  537.2 6.2 fusion.174
  543.4 7.7 bitcast_convert_fusion
  551.2 10.5 %convolution_bitcast_fusion = f32[3072,768]{1,0:T(8,128)} fusion(bf16[2,384,3072]{2,1,0:T(8,128)(2,1)} %get-tuple-element.122, bf16[2,384,768]{2,1,0:T(8,128)(2,1)} %param.33), kind=kOutput, calls=%fused_computation.140 | convolution fusion | flops 3623878656 | bytes 15335424 | tf_op jit(solution)/shard_map/rlf,rld->fd/dot_general | solution.py:143
  561.7 9.2 convolution_bitcast_fusion.1
  571.7 8.8 add_convert_fusion.3
  580.9 21.5 %psum.87 = bf16[2,192]{1,0:T(2,128)(2,1)S(1)} all-reduce(bf16[2,192]{1,0:T(2,128)(2,1)S(1)} %slice_reduce_fusion), channel_id=1, replica_groups=mesh['dp'=8,'th'=2,'tw'=2] {'dp'}, use_global_device_ids=true, to_apply=%region_29.30 | all-reduce | flops 384 | bytes 1536 | tf_op jit(solution)/shard_map/psum | solution.py:178
  603.0 20.8 %all-reduce.8.cloned.1.call-done = (bf16[3,768,192]{1,2,0:T(8,128)(2,1)}, bf16[192,768]{1,0:T(8,128)(2,1)}) async-done(((bf16[3,768,192]{1,2,0:T(8,128)(2,1)}, bf16[192,768]{1,0:T(8,128)(2,1)}), (bf16[3,768,192]{1,2,0:T(8,128)(2,1)}, bf16[192,768]{1,0:T(8,128)(2,1)})) %all-reduce.8.cloned.1.call-update) | async-done | bytes 1179664 | tf_op jit(solution)/shard_map/psum | solution.py:177
  625.6 2.5 convert_element_type.154
  628.1 45.2 %reduce-scatter.5.cloned.1.call-done = bf16[2,384,768]{2,1,0:T(8,128)(2,1)} async-done(((bf16[2,1536,768]{2,1,0:T(8,128)(2,1)}), bf16[2,384,768]{2,1,0:T(8,128)(2,1)}) %reduce-scatter.5.cloned.1.call-update) | async-done | bytes 1179664 | tf_op jit(solution)/shard_map/reduce_scatter | solution.py:171
  675.6 2.7 fusion.163
  678.4 3.0 convert_reduce_fusion.3
  681.4 42.5 %all-reduce = (f32[768]{0:T(1024)}, f32[768]{0:T(1024)}, f32[768]{0:T(1024)}, f32[768]{0:T(1024)}, f32[768]{0:T(1024)}, /*index=5*/f32[3072]{0:T(1024)}, f32[768]{0:T(1024)}) all-reduce(f32[768]{0:T(1024)S(1)} %get-tuple-element.81, f32[768]{0:T(1024)S(1)} %get-tuple-element.85, ...), channel_id=1, replica_groups=mesh['dp'=8,'th'=2,'tw'=2] {'dp','th','tw'}, use_global_device_ids=true, to_apply=%region_24.25 | all-reduce | flops 7680 | bytes 61440 | tf_op jit(solution)/shard_map/psum | solution.py:181
  724.0 262.5 %all-reduce.6.cloned.1.call-done = (f32[768,3072]{1,0:T(8,128)}, f32[3072,768]{1,0:T(8,128)}) async-done(((f32[768,3072]{1,0:T(8,128)}, f32[3072,768]{1,0:T(8,128)}), (f32[768,3072]{1,0:T(8,128)}, f32[3072,768]{1,0:T(8,128)})) %all-reduce.6.cloned.1.call-update) | async-done | bytes 18874384 | tf_op jit(solution)/shard_map/psum | solution.py:181
  986.5 8.8 copy.59
  995.2 3.7 copy.60
  (212 shorter events, 65.0 us)
Async XLA Ops:
  7.2 47.7 %copy-start = (bf16[3,768,192]{1,2,0:T(8,128)(2,1)S(1)}, bf16[3,768,192]{1,2,0:T(8,128)(2,1)}, u32[]{:S(2)}) copy-start(bf16[3,768,192]{1,2,0:T(8,128)(2,1)} %param.23) | copy-start | bytes 2654212
  7.2 7.5 copy-start.48
  7.2 47.7 %all-gather.3.cloned.1.call-start = ((), (), s32[]{:S(2)}) async-start(), calls=%async_computation.2 | async-start | bytes 5898240 | tf_op jit(solution)/shard_map/all_gather | solution.py:119
  8.8 2.3 copy-start.32
  14.6 159.3 %reduce-scatter.3.cloned.1.call-start = ((), (), s32[]{:S(2)}) async-start(), calls=%async_computation.3 | async-start | bytes 5898240 | tf_op jit(solution)/shard_map/reduce_scatter | solution.py:126
  14.8 46.8 %copy-start.20 = (s32[2,1536]{1,0:T(2,128)S(1)}, s32[2,1536]{1,0:T(2,128)}, u32[]{:S(2)}) copy-start(s32[2,1536]{1,0:T(2,128)} %param.20) | copy-start | bytes 36868
  120.8 5.0 copy-start.17
  120.9 53.0 %copy-start.5 = (bf16[2,384,768]{2,1,0:T(8,128)(2,1)S(1)}, bf16[2,384,768]{2,1,0:T(8,128)(2,1)}, u32[]{:S(2)}) copy-start(bf16[2,384,768]{2,1,0:T(8,128)(2,1)} %param.19) | copy-start | bytes 3538948
  120.9 53.0 %copy-start.21 = (f32[768]{0:T(1024)S(1)}, f32[768]{0:T(1024)}, u32[]{:S(2)}) copy-start(f32[768]{0:T(1024)} %param.26) | copy-start | bytes 9220
  125.8 51.8 %copy-start.25 = (f32[768]{0:T(1024)S(1)}, f32[768]{0:T(1024)}, u32[]{:S(2)}) copy-start(f32[768]{0:T(1024)} %param.27) | copy-start | bytes 9220
  125.8 51.8 %copy-start.30 = (f32[768]{0:T(1024)S(1)}, f32[768]{0:T(1024)}, u32[]{:S(2)}) copy-start(f32[768]{0:T(1024)} %param.28) | copy-start | bytes 9220
  125.8 51.8 %copy-start.45 = (f32[3072]{0:T(1024)S(1)}, f32[3072]{0:T(1024)}, u32[]{:S(2)}) copy-start(f32[3072]{0:T(1024)} %param.30) | copy-start | bytes 36868
  125.8 147.5 %all-gather.5.cloned.1.call-start = ((), (), s32[]{:S(2)}) async-start(), calls=%async_computation.4 | async-start | bytes 5898240 | tf_op jit(solution)/shard_map/all_gather | solution.py:160
  173.8 3.8 copy-start.7
  175.7 57.2 %copy-start.23 = (f32[2,384]{1,0:T(2,128)}, f32[2,384]{1,0:T(2,128)S(1)}, u32[]{:S(2)}) copy-start(f32[2,384]{1,0:T(2,128)S(1)} %broadcast_multiply_fusion) | copy-start | bytes 9220
  177.7 55.3 %copy-start.27 = (f32[2,384]{1,0:T(2,128)}, f32[2,384]{1,0:T(2,128)S(1)}, u32[]{:S(2)}) copy-start(f32[2,384]{1,0:T(2,128)S(1)} %fusion.183) | copy-start | bytes 9220
  186.8 23.4 %copy-start.15 = (bf16[2,384,768]{2,1,0:T(8,128)(2,1)S(1)}, bf16[2,384,768]{2,1,0:T(8,128)(2,1)}, u32[]{:S(2)}) copy-start(bf16[2,384,768]{2,1,0:T(8,128)(2,1)} %param.33) | copy-start | bytes 3538948
  230.9 4.8 copy-start.9
  230.9 4.8 copy-start.35
  232.9 40.4 %copy-start.29 = (bf16[192,768]{1,0:T(8,128)(2,1)S(1)}, bf16[192,768]{1,0:T(8,128)(2,1)}, u32[]{:S(2)}) copy-start(bf16[192,768]{1,0:T(8,128)(2,1)} %param.25) | copy-start | bytes 884740
  232.9 45.4 %copy-start.39 = (f32[2,384]{1,0:T(2,128)}, f32[2,384]{1,0:T(2,128)S(1)}, u32[]{:S(2)}) copy-start(f32[2,384]{1,0:T(2,128)S(1)} %negate_multiply_fusion.2) | copy-start | bytes 9220
  235.7 388.1 %all-reduce.8.cloned.1.call-start = ((), (), s32[]{:S(2)}) async-start(), calls=%async_computation.7 | async-start | bytes 2359296 | tf_op jit(solution)/shard_map/psum | solution.py:177
  278.7 2.8 copy-start.1
  281.7 4.9 copy-start.12
  285.6 3.6 copy-start.2
  291.7 7.7 copy-start.4
  294.2 4.3 copy-start.3
  389.9 14.2 %copy-start.13 = (bf16[3,64,512]{2,1,0:T(8,128)(2,1)S(1)}, bf16[3,64,512]{2,1,0:T(8,128)(2,1)}, u32[]{:S(2)}) copy-start(bf16[3,64,512]{2,1,0:T(8,128)(2,1)} %fusion.377) | copy-start | bytes 589828 | tf_op jit(solution)/shard_map/while
  389.9 14.2 %copy-start.14 = (bf16[3,64,512]{2,1,0:T(8,128)(2,1)S(1)}, bf16[3,64,512]{2,1,0:T(8,128)(2,1)}, u32[]{:S(2)}) copy-start(bf16[3,64,512]{2,1,0:T(8,128)(2,1)} %fusion.378) | copy-start | bytes 589828 | tf_op jit(solution)/shard_map/while
  405.6 2.8 copy-start.1
  408.6 4.9 copy-start.12
  412.5 3.6 copy-start.2
  418.6 7.7 copy-start.4
  421.0 4.3 copy-start.3
  516.7 14.2 %copy-start.13 = (bf16[3,64,512]{2,1,0:T(8,128)(2,1)S(1)}, bf16[3,64,512]{2,1,0:T(8,128)(2,1)}, u32[]{:S(2)}) copy-start(bf16[3,64,512]{2,1,0:T(8,128)(2,1)} %fusion.377) | copy-start | bytes 589828 | tf_op jit(solution)/shard_map/while
  516.8 14.2 %copy-start.14 = (bf16[3,64,512]{2,1,0:T(8,128)(2,1)S(1)}, bf16[3,64,512]{2,1,0:T(8,128)(2,1)}, u32[]{:S(2)}) copy-start(bf16[3,64,512]{2,1,0:T(8,128)(2,1)} %fusion.378) | copy-start | bytes 589828 | tf_op jit(solution)/shard_map/while
  532.5 4.7 copy-start.18
  543.3 130.0 %reduce-scatter.5.cloned.1.call-start = ((), (), s32[]{:S(2)}) async-start(), calls=%async_computation.5 | async-start | bytes 5898240 | tf_op jit(solution)/shard_map/reduce_scatter | solution.py:171
  551.1 435.4 %all-reduce.6.cloned.1.call-start = ((), (), s32[]{:S(2)}) async-start(), calls=%async_computation.6 | async-start | bytes 37748736 | tf_op jit(solution)/shard_map/psum | solution.py:181
  551.1 10.6 %copy-start.6 = (bf16[2,384,768]{2,1,0:T(8,128)(2,1)S(1)}, bf16[2,384,768]{2,1,0:T(8,128)(2,1)}, u32[]{:S(2)}) copy-start(bf16[2,384,768]{2,1,0:T(8,128)(2,1)} %param.19) | copy-start | bytes 3538948
  551.1 10.6 %copy-start.8 = (bf16[2,384,768]{2,1,0:T(8,128)(2,1)S(1)}, bf16[2,384,768]{2,1,0:T(8,128)(2,1)}, u32[]{:S(2)}) copy-start(bf16[2,384,768]{2,1,0:T(8,128)(2,1)} %reduce-scatter.3.cloned.1.call-done) | copy-start | bytes 3538948
  551.2 10.5 %copy-start.22 = (f32[768]{0:T(1024)S(1)}, f32[768]{0:T(1024)}, u32[]{:S(2)}) copy-start(f32[768]{0:T(1024)} %param.26) | copy-start | bytes 9220
  551.2 10.5 %copy-start.24 = (f32[2,384]{1,0:T(2,128)S(1)}, f32[2,384]{1,0:T(2,128)}, u32[]{:S(2)}) copy-start(f32[2,384]{1,0:T(2,128)} %copy-done.23) | copy-start | bytes 9220
  551.2 10.5 %copy-start.26 = (f32[768]{0:T(1024)S(1)}, f32[768]{0:T(1024)}, u32[]{:S(2)}) copy-start(f32[768]{0:T(1024)} %param.27) | copy-start | bytes 9220
  551.2 10.5 %copy-start.28 = (f32[2,384]{1,0:T(2,128)S(1)}, f32[2,384]{1,0:T(2,128)}, u32[]{:S(2)}) copy-start(f32[2,384]{1,0:T(2,128)} %copy-done.27) | copy-start | bytes 9220
  551.2 10.5 %copy-start.31 = (f32[768]{0:T(1024)S(1)}, f32[768]{0:T(1024)}, u32[]{:S(2)}) copy-start(f32[768]{0:T(1024)} %param.28) | copy-start | bytes 9220
  571.0 0.7 copy-start.49
  571.7 8.8 copy-start.19
  580.5 92.9 %copy-start.33 = (f32[2,384]{1,0:T(2,128)S(1)}, f32[2,384]{1,0:T(2,128)}, u32[]{:S(2)}) copy-start(f32[2,384]{1,0:T(2,128)} %copy-done.32) | copy-start | bytes 9220
  580.5 92.9 %copy-start.34 = (f32[768]{0:T(1024)S(1)}, f32[768]{0:T(1024)}, u32[]{:S(2)}) copy-start(f32[768]{0:T(1024)} %param.21) | copy-start | bytes 9220
  580.5 95.1 %copy-start.42 = (f32[2,384]{1,0:T(2,128)S(1)}, f32[2,384]{1,0:T(2,128)}, u32[]{:S(2)}) copy-start(f32[2,384]{1,0:T(2,128)} %copy-done.41) | copy-start | bytes 9220
  580.5 95.1 %copy-start.38 = (f32[2,384]{1,0:T(2,128)S(1)}, f32[2,384]{1,0:T(2,128)}, u32[]{:S(2)}) copy-start(f32[2,384]{1,0:T(2,128)} %copy-done.37) | copy-start | bytes 9220
  580.9 97.5 %copy-start.36 = (f32[2,384]{1,0:T(2,128)S(1)}, f32[2,384]{1,0:T(2,128)}, u32[]{:S(2)}) copy-start(f32[2,384]{1,0:T(2,128)} %copy-done.35) | copy-start | bytes 9220
  580.9 97.5 %copy-start.40 = (f32[2,384]{1,0:T(2,128)S(1)}, f32[2,384]{1,0:T(2,128)}, u32[]{:S(2)}) copy-start(f32[2,384]{1,0:T(2,128)} %copy-done.39) | copy-start | bytes 9220
  673.3 5.1 copy-start.10
  673.3 5.1 copy-start.11
  673.3 5.1 copy-start.16
  678.3 3.1 copy-start.43
  678.3 3.1 copy-start.44
  678.3 3.1 copy-start.46
  678.4 3.1 copy-start.47
  986.5 8.8 slice-start
  986.5 8.8 slice-start.1
  986.5 8.8 slice-start.2
  (2 other events, 1.2 us)
Sparse Core Ops, SparseCore 0:
  14.7 40.1 all-gather.2
  126.0 47.8 reduce-scatter.2
  235.8 37.4 all-gather.4
  543.5 80.2 all-reduce.7
  626.2 47.1 reduce-scatter.4
  681.3 305.1 all-reduce.5
where the time goes:
time: 1010 us
  waiting for transfers between devices  454 us (45%)
  matrix products  354 us (35%)
  other arithmetic  75.9 us (8%)
  blocking collectives  64 us (6%)
  local copies, waits for them, and re-layouts  40.5 us (4%)
  between operations  14.8 us (1%)
    psum x1, waiting for transfers between devices, body(): lax.psum((grad_gain_one, grad_shift_one, grad_b_out, grad_gain_two, grad_...  263 us
    dot_general x6, matrix products, row_backward(): jnp.einsum('hqk,khe->qhe', score_grad, key_rows, preferred_element_type=j...  89.1 us
    dot_general x6, matrix products, row_backward(): jnp.einsum('hqk,qhe->khe', score_grad, query_block, preferred_element_typ...  87.3 us
    reduce_scatter x1, waiting for transfers between devices, body(): lax.psum_scatter(partial_out.astype(jnp.bfloat16), ('th', 'tw'), scatter_...  47.9 us
    reduce_scatter x1, waiting for transfers between devices, body(): lax.psum_scatter(grad_normed.astype(jnp.bfloat16), ('th', 'tw'), scatter_...  45.2 us
    psum x1, blocking collectives, body(): lax.psum((grad_gain_one, grad_shift_one, grad_b_out, grad_gain_two, grad_...  42.5 us
    all_gather x1, waiting for transfers between devices, body(): gathered = lax.all_gather(normed_low, ('th', 'tw'), axis=1, tiled=True)  40.1 us
    all_gather x1, waiting for transfers between devices, body(): grad_whole = lax.all_gather(grad_branch, ('th', 'tw'), axis=1, tiled=True)  37.6 us
  transfers between devices with their start and end apart: 6, of which 6 were waited for; matrix products, arithmetic and copies ran while one was open for 5% of the time, Pallas kernels for 0%

commit v1 on v0

--- a/solution.py
+++ b/solution.py
@@ -179,18 +179,21 @@
         lax.psum(grad_w_out.astype(jnp.bfloat16), "dp").astype(jnp.float32),
     )
     shared = lax.psum(
-        (
-            grad_gain_one,
-            grad_shift_one,
-            grad_b_out,
-            grad_gain_two,
-            grad_shift_two,
-            grad_w_up,
-            grad_b_up,
-            grad_w_down,
-            grad_b_down,
+        lax.psum(
+            (
+                grad_gain_one,
+                grad_shift_one,
+                grad_b_out,
+                grad_gain_two,
+                grad_shift_two,
+                grad_w_up,
+                grad_b_up,
+                grad_w_down,
+                grad_b_down,
+            ),
+            ("th", "tw"),
         ),
-        ("dp", "th", "tw"),
+        "dp",
     )
     return (
         block_out.astype(jnp.bfloat16),

time: 1010 us -> 1330 us (1.32)
  waiting for transfers between devices: 454 us -> 749 us
    psum x0 -> x1, waiting for transfers between devices: none -> 512 us  [body(): lax.psum(lax.psum((grad_gain_one, grad_shift_one, grad_b_out, grad_gain_t...]
    psum x1, waiting for transfers between devices: 263 us -> 34.6 us  [body(): lax.psum((grad_gain_one, grad_shift_one, grad_b_out, grad_gain_two, grad_...]
    psum x0 -> x1, blocking collectives: none -> 41.6 us  [body(): lax.psum(lax.psum((grad_gain_one, grad_shift_one, grad_b_out, grad_gain_t...]
    psum x1, waiting for transfers between devices: 20.8 us -> 51.6 us  [body(): lax.psum(grad_w_qkv.astype(jnp.bfloat16), 'dp').astype(jnp.float32)]
    psum x1, blocking collectives: 42.5 us -> 12.3 us  [body(): lax.psum((grad_gain_one, grad_shift_one, grad_b_out, grad_gain_two, grad_...]
    all_gather x1, waiting for transfers between devices: 37.6 us -> 17.3 us  [body(): grad_whole = lax.all_gather(grad_branch, ('th', 'tw'), axis=1, tiled=True)]
  transfers between devices with their start and end apart: 6 -> 7, of which waited for: 6 -> 7; matrix products, arithmetic and copies ran while one was open for 5% -> 23% of each run, Pallas kernels for 0% -> 0%
where the time goes in v1:
time: 1330 us
  waiting for transfers between devices  749 us (56%)
  matrix products  359 us (27%)
  other arithmetic  75.9 us (6%)
  blocking collectives  75.6 us (6%)
  local copies, waits for them, and re-layouts  41.5 us (3%)
  between operations  14.8 us (1%)
    psum x1, waiting for transfers between devices, body(): lax.psum(lax.psum((grad_gain_one, grad_shift_one, grad_b_out, grad_gain_t...  512 us
    dot_general x6, matrix products, row_backward(): jnp.einsum('hqk,khe->qhe', score_grad, key_rows, preferred_element_type=j...  91.6 us
    dot_general x6, matrix products, row_backward(): jnp.einsum('hqk,qhe->khe', score_grad, query_block, preferred_element_typ...  90 us
    psum x1, waiting for transfers between devices, body(): lax.psum(grad_w_qkv.astype(jnp.bfloat16), 'dp').astype(jnp.float32)  51.6 us
    reduce_scatter x1, waiting for transfers between devices, body(): lax.psum_scatter(partial_out.astype(jnp.bfloat16), ('th', 'tw'), scatter_...  47.9 us
    reduce_scatter x1, waiting for transfers between devices, body(): lax.psum_scatter(grad_normed.astype(jnp.bfloat16), ('th', 'tw'), scatter_...  45.4 us
    psum x1, blocking collectives, body(): lax.psum(lax.psum((grad_gain_one, grad_shift_one, grad_b_out, grad_gain_t...  41.6 us
    all_gather x1, waiting for transfers between devices, body(): gathered = lax.all_gather(normed_low, ('th', 'tw'), axis=1, tiled=True)  40.1 us
  transfers between devices with their start and end apart: 7, of which 7 were waited for; matrix products, arithmetic and copies ran while one was open for 23% of the time, Pallas kernels for 0%

profile of v1, /device:TPU:0, one launch (start us, length us, event | category | flops | bytes accessed | tf_op | source)
XLA Modules:
  0.0 1326.9 jit_solution(14180979223463587359)
XLA Ops:
  11.7 2.8 fusion.160
  14.8 40.1 %all-gather.3.cloned.1.call-done = bf16[2,1536,768]{2,1,0:T(8,128)(2,1)} async-done(((bf16[2,384,768]{2,1,0:T(8,128)(2,1)}), bf16[2,1536,768]{2,1,0:T(8,128)(2,1)}) %all-gather.3.cloned.1.call-update) | async-done | bytes 4718608 | tf_op jit(solution)/shard_map/all_gather | solution.py:119
  54.9 6.7 fusion.154
  61.6 59.1 %while.22 = (s32[]{:T(128)}, bf16[2,1536,192]{1,2,0:T(8,128)(2,1)S(1)}, f32[2,3,1536]{2,1,0:T(4,128)S(1)}, bf16[2,3,1536,192]{2,3,1,0:T(8,128)(2,1)}, s32[2,1536...) while((s32[]{:T(128)}, bf16[2,1536,192]{1,2,0:T(8,128)(2,1)S(1)}, ...), condition=%wide.region_9.10_spmd, body=%wide.region_2.9_spmd.sunk | while | flops 1901302272 | bytes 107581632 | solution.py:123
  68.6 2.8 fusion.320
  71.4 3.5 fusion.321
  78.9 5.2 fusion.324
  84.1 3.5 fusion.326
  87.6 3.5 fusion.325
  97.8 2.8 fusion.320
  100.6 3.5 fusion.321
  108.2 5.2 fusion.324
  113.3 3.5 fusion.326
  116.9 3.5 fusion.325
  120.7 4.9 convolution_convert_fusion
  125.8 47.9 %reduce-scatter.3.cloned.1.call-done = bf16[2,384,768]{2,1,0:T(8,128)(2,1)} async-done(((bf16[2,1536,768]{2,1,0:T(8,128)(2,1)}), bf16[2,384,768]{2,1,0:T(8,128)(2,1)}) %reduce-scatter.3.cloned.1.call-update) | async-done | bytes 1179664 | tf_op jit(solution)/shard_map/reduce_scatter | solution.py:126
  177.5 9.2 fusion.165
  186.7 23.4 %multiply_convert_fusion.3 = (bf16[2,384,3072]{2,1,0:T(8,128)(2,1)}, f32[2,384,3072]{2,1,0:T(8,128)}) fusion(f32[2,384,3072]{2,1,0:T(8,128)S(1)} %get-tuple-element.173, f32[3072]{0:T(1024)S(1)} %copy-done.44, u8[384,3072]{1,0:T(8,128)(4,1)S(1)} %get-tuple-element.78, u8[384,3072]{1,0:T(8,128)(4,1)S(1)} %get-tuple-element.77), kind=kLoop, calls=%fused_computation.126 | loop fusion | flops 167510016 | bytes 25964544 | tf_op jit(solution)/shard_map/convert_element_type | solution.py:138
  210.1 12.5 convert_reduce_fusion
  222.6 8.1 fusion.185
  232.7 2.7 convert_reduce_fusion.4
  236.0 10.8 convolution_bitcast_fusion
  246.7 9.0 convolution_bitcast_fusion.1
  255.8 17.3 %all-gather.5.cloned.1.call-done = bf16[2,1536,768]{2,1,0:T(8,128)(2,1)} async-done(((bf16[2,384,768]{2,1,0:T(8,128)(2,1)}), bf16[2,1536,768]{2,1,0:T(8,128)(2,1)}) %all-gather.5.cloned.1.call-update) | async-done | bytes 4718608 | tf_op jit(solution)/shard_map/all_gather | solution.py:160
  273.1 5.0 convolution_convert_fusion.1
  278.1 267.2 %while.23 = (s32[]{:T(128)}, bf16[2,3,1536,192]{2,3,1,0:T(8,128)(2,1)}, bf16[2,3,1536,192]{2,3,1,0:T(8,128)(2,1)}, s32[2,1536]{1,0:T(2,128)S(1)}, f32[2,3,1536]{...) while((s32[]{:T(128)}, ...), condition=%wide.region_19.20_spmd, body=%wide.region_15.19_spmd.sunk | while | flops 4682926080 | bytes 364640672 | solution.py:167
  286.2 2.7 copy-done.2
  293.8 4.2 copy-done.3
  299.9 4.9 fusion.371
  304.8 15.1 %fusion.377 = bf16[3,64,512]{2,1,0:T(8,128)(2,1)} fusion(bf16[1536,3,64]{0,2,1:T(8,128)(2,1)S(1)} %bitcast.312, f32[3,512,1536]{2,1,0:T(8,128)} %copy-done.4, f32[3,512,1536]{2,1,0:T(8,128)} %fusion.371), kind=kOutput, calls=%fused_computation.94.clone.1 | convolution fusion | flops 320965632 | bytes 19660800 | tf_op jit(solution)/shard_map/while/body/eval_jaxpr/hqk,khe->qhe/dot_general | solution.py:82
  320.0 16.2 %fusion.372 = f32[3,64,1536]{2,1,0:T(8,128)} fusion(bf16[512,3,64]{0,2,1:T(8,128)(2,1)} %bitcast.323, f32[3,512,1536]{2,1,0:T(8,128)} %copy-done.4, f32[3,512,1536]{2,1,0:T(8,128)} %fusion.371), kind=kOutput, calls=%fused_computation.63.clone.1 | convolution fusion | flops 320867328 | bytes 20250624 | tf_op jit(solution)/shard_map/while/body/eval_jaxpr/hqk,qhe->khe/dot_general | solution.py:86
  336.1 5.0 fusion.375
  341.2 14.5 %fusion.379 = bf16[3,64,512]{2,1,0:T(8,128)(2,1)S(1)} fusion(bf16[1536,3,64]{0,2,1:T(8,128)(2,1)S(1)} %bitcast.313, f32[3,512,1536]{2,1,0:T(8,128)} %copy-done.3, f32[3,512,1536]{2,1,0:T(8,128)} %fusion.375), kind=kOutput, calls=%fused_computation.92.clone.1 | convolution fusion | flops 320965632 | bytes 19660800 | tf_op jit(solution)/shard_map/while/body/eval_jaxpr/hqk,khe->qhe/dot_general | solution.py:82
  355.6 4.9 fusion.373
  360.6 15.5 %fusion.378 = bf16[3,64,512]{2,1,0:T(8,128)(2,1)} fusion(bf16[1536,3,64]{0,2,1:T(8,128)(2,1)S(1)} %bitcast.314, f32[3,512,1536]{2,1,0:T(8,128)} %copy-done.2, f32[3,512,1536]{2,1,0:T(8,128)} %fusion.373), kind=kOutput, calls=%fused_computation.93.clone.1 | convolution fusion | flops 320965632 | bytes 19660800 | tf_op jit(solution)/shard_map/while/body/eval_jaxpr/hqk,khe->qhe/dot_general | solution.py:82
  376.1 15.4 %fusion.374 = f32[3,64,1536]{2,1,0:T(8,128)} fusion(bf16[512,3,64]{0,2,1:T(8,128)(2,1)S(1)} %bitcast.321, f32[3,512,1536]{2,1,0:T(8,128)} %copy-done.2, f32[3,512,1536]{2,1,0:T(8,128)} %fusion.373), kind=kOutput, calls=%fused_computation.67.clone.1 | convolution fusion | flops 320867328 | bytes 20250624 | tf_op jit(solution)/shard_map/while/body/eval_jaxpr/hqk,qhe->khe/dot_general | solution.py:86
  391.5 14.2 %fusion.376 = bf16[3,64,1536]{2,1,0:T(8,128)(2,1)S(1)} fusion(f32[3,64,1536]{2,1,0:T(8,128)} %fusion.372, f32[3,64,1536]{2,1,0:T(8,128)} %fusion.374, bf16[512,3,64]{0,2,1:T(8,128)(2,1)S(1)} %bitcast.319, f32[3,512,1536]{2,1,0:T(8,128)} %copy-done.3, f32[3,512,1536]{2,1,0:T(8,128)} %fusion.375), kind=kOutput, calls=%fused_computation.79.clone.1 | convolution fusion | flops 321752064 | bytes 22020096 | tf_op jit(solution)/shard_map/while/body/eval_jaxpr/hqk,qhe->khe/dot_general | solution.py:86
  415.1 2.7 copy-done.2
  422.8 4.3 copy-done.3
  428.9 4.9 fusion.371
  433.9 16.3 %fusion.377 = bf16[3,64,512]{2,1,0:T(8,128)(2,1)} fusion(bf16[1536,3,64]{0,2,1:T(8,128)(2,1)S(1)} %bitcast.312, f32[3,512,1536]{2,1,0:T(8,128)} %copy-done.4, f32[3,512,1536]{2,1,0:T(8,128)} %fusion.371), kind=kOutput, calls=%fused_computation.94.clone.1 | convolution fusion | flops 320965632 | bytes 19660800 | tf_op jit(solution)/shard_map/while/body/eval_jaxpr/hqk,khe->qhe/dot_general | solution.py:82
  450.2 15.4 %fusion.372 = f32[3,64,1536]{2,1,0:T(8,128)} fusion(bf16[512,3,64]{0,2,1:T(8,128)(2,1)} %bitcast.323, f32[3,512,1536]{2,1,0:T(8,128)} %copy-done.4, f32[3,512,1536]{2,1,0:T(8,128)} %fusion.371), kind=kOutput, calls=%fused_computation.63.clone.1 | convolution fusion | flops 320867328 | bytes 20250624 | tf_op jit(solution)/shard_map/while/body/eval_jaxpr/hqk,qhe->khe/dot_general | solution.py:86
  465.6 5.0 fusion.375
  470.6 14.5 %fusion.379 = bf16[3,64,512]{2,1,0:T(8,128)(2,1)S(1)} fusion(bf16[1536,3,64]{0,2,1:T(8,128)(2,1)S(1)} %bitcast.313, f32[3,512,1536]{2,1,0:T(8,128)} %copy-done.3, f32[3,512,1536]{2,1,0:T(8,128)} %fusion.375), kind=kOutput, calls=%fused_computation.92.clone.1 | convolution fusion | flops 320965632 | bytes 19660800 | tf_op jit(solution)/shard_map/while/body/eval_jaxpr/hqk,khe->qhe/dot_general | solution.py:82
  485.1 5.0 fusion.373
  490.1 15.7 %fusion.378 = bf16[3,64,512]{2,1,0:T(8,128)(2,1)} fusion(bf16[1536,3,64]{0,2,1:T(8,128)(2,1)S(1)} %bitcast.314, f32[3,512,1536]{2,1,0:T(8,128)} %copy-done.2, f32[3,512,1536]{2,1,0:T(8,128)} %fusion.373), kind=kOutput, calls=%fused_computation.93.clone.1 | convolution fusion | flops 320965632 | bytes 19660800 | tf_op jit(solution)/shard_map/while/body/eval_jaxpr/hqk,khe->qhe/dot_general | solution.py:82
  505.8 14.6 %fusion.374 = f32[3,64,1536]{2,1,0:T(8,128)} fusion(bf16[512,3,64]{0,2,1:T(8,128)(2,1)S(1)} %bitcast.321, f32[3,512,1536]{2,1,0:T(8,128)} %copy-done.2, f32[3,512,1536]{2,1,0:T(8,128)} %fusion.373), kind=kOutput, calls=%fused_computation.67.clone.1 | convolution fusion | flops 320867328 | bytes 20250624 | tf_op jit(solution)/shard_map/while/body/eval_jaxpr/hqk,qhe->khe/dot_general | solution.py:86
  520.4 14.3 %fusion.376 = bf16[3,64,1536]{2,1,0:T(8,128)(2,1)S(1)} fusion(f32[3,64,1536]{2,1,0:T(8,128)} %fusion.372, f32[3,64,1536]{2,1,0:T(8,128)} %fusion.374, bf16[512,3,64]{0,2,1:T(8,128)(2,1)S(1)} %bitcast.319, f32[3,512,1536]{2,1,0:T(8,128)} %copy-done.3, f32[3,512,1536]{2,1,0:T(8,128)} %fusion.375), kind=kOutput, calls=%fused_computation.79.clone.1 | convolution fusion | flops 321752064 | bytes 22020096 | tf_op jit(solution)/shard_map/while/body/eval_jaxpr/hqk,qhe->khe/dot_general | solution.py:86
  545.3 4.7 fusion.177
  550.0 6.2 fusion.174
  556.3 7.7 bitcast_convert_fusion
  564.1 34.6 %all-reduce.11.cloned.1.call-done = (f32[768,3072]{1,0:T(8,128)}, f32[3072,768]{1,0:T(8,128)}) async-done(((f32[768,3072]{1,0:T(8,128)}, f32[3072,768]{1,0:T(8,128)}), (f32[768,3072]{1,0:T(8,128)}, f32[3072,768]{1,0:T(8,128)})) %all-reduce.11.cloned.1.call-update) | async-done | bytes 18874384 | tf_op jit(solution)/shard_map/psum | solution.py:182
  600.3 8.8 add_convert_fusion.3
  609.6 21.7 %psum.152 = bf16[2,192]{1,0:T(2,128)(2,1)S(1)} all-reduce(bf16[2,192]{1,0:T(2,128)(2,1)S(1)} %slice_reduce_fusion), channel_id=1, replica_groups=mesh['dp'=8,'th'=2,'tw'=2] {'dp'}, use_global_device_ids=true, to_apply=%region_31.32 | all-reduce | flops 384 | bytes 1536 | tf_op jit(solution)/shard_map/psum | solution.py:178
  631.8 51.6 %all-reduce.13.cloned.1.call-done = (bf16[3,768,192]{1,2,0:T(8,128)(2,1)}, bf16[192,768]{1,0:T(8,128)(2,1)}) async-done(((bf16[3,768,192]{1,2,0:T(8,128)(2,1)}, bf16[192,768]{1,0:T(8,128)(2,1)}), (bf16[3,768,192]{1,2,0:T(8,128)(2,1)}, bf16[192,768]{1,0:T(8,128)(2,1)})) %all-reduce.13.cloned.1.call-update) | async-done | bytes 1179664 | tf_op jit(solution)/shard_map/psum | solution.py:177
  685.2 2.5 convert_element_type.154
  687.7 45.4 %reduce-scatter.5.cloned.1.call-done = bf16[2,384,768]{2,1,0:T(8,128)(2,1)} async-done(((bf16[2,1536,768]{2,1,0:T(8,128)(2,1)}), bf16[2,384,768]{2,1,0:T(8,128)(2,1)}) %reduce-scatter.5.cloned.1.call-update) | async-done | bytes 1179664 | tf_op jit(solution)/shard_map/reduce_scatter | solution.py:171
  735.4 2.7 fusion.163
  738.3 3.0 convert_reduce_fusion.3
  741.2 12.3 all-reduce.2
  753.6 41.6 %all-reduce = (f32[768]{0:T(1024)}, f32[768]{0:T(1024)}, f32[768]{0:T(1024)}, f32[768]{0:T(1024)}, f32[768]{0:T(1024)}, /*index=5*/f32[3072]{0:T(1024)}, f32[768]{0:T(1024)}) all-reduce(f32[768]{0:T(1024)S(1)} %get-tuple-element.118, f32[768]{0:T(1024)S(1)} %get-tuple-element.119, ...), channel_id=1, replica_groups=mesh['dp'=8,'th'=2,'tw'=2] {'dp'}, use_global_device_ids=true, to_apply=%region_25.26 | all-reduce | flops 7680 | bytes 61440 | tf_op jit(solution)/shard_map/psum | solution.py:181
  795.2 512.1 %all-reduce.9.cloned.1.call-done = (f32[768,3072]{1,0:T(8,128)}, f32[3072,768]{1,0:T(8,128)}) async-done(((f32[768,3072]{1,0:T(8,128)}, f32[3072,768]{1,0:T(8,128)}), (f32[768,3072]{1,0:T(8,128)}, f32[3072,768]{1,0:T(8,128)})) %all-reduce.9.cloned.1.call-update) | async-done | bytes 18874384 | tf_op jit(solution)/shard_map/psum | solution.py:181
  1307.4 8.8 copy.61
  1316.2 3.7 copy.62
  (214 shorter events, 71.3 us)
Async XLA Ops:
  7.2 47.7 %copy-start = (bf16[3,768,192]{1,2,0:T(8,128)(2,1)S(1)}, bf16[3,768,192]{1,2,0:T(8,128)(2,1)}, u32[]{:S(2)}) copy-start(bf16[3,768,192]{1,2,0:T(8,128)(2,1)} %param.23) | copy-start | bytes 2654212
  7.2 7.5 copy-start.47
  7.2 47.7 %all-gather.3.cloned.1.call-start = ((), (), s32[]{:S(2)}) async-start(), calls=%async_computation.2 | async-start | bytes 5898240 | tf_op jit(solution)/shard_map/all_gather | solution.py:119
  8.8 2.3 copy-start.31
  14.6 159.1 %reduce-scatter.3.cloned.1.call-start = ((), (), s32[]{:S(2)}) async-start(), calls=%async_computation.3 | async-start | bytes 5898240 | tf_op jit(solution)/shard_map/reduce_scatter | solution.py:126
  14.8 46.8 %copy-start.20 = (s32[2,1536]{1,0:T(2,128)S(1)}, s32[2,1536]{1,0:T(2,128)}, u32[]{:S(2)}) copy-start(s32[2,1536]{1,0:T(2,128)} %param.20) | copy-start | bytes 36868
  120.7 5.0 copy-start.17
  120.7 53.0 %copy-start.5 = (bf16[2,384,768]{2,1,0:T(8,128)(2,1)S(1)}, bf16[2,384,768]{2,1,0:T(8,128)(2,1)}, u32[]{:S(2)}) copy-start(bf16[2,384,768]{2,1,0:T(8,128)(2,1)} %param.19) | copy-start | bytes 3538948
  120.7 53.0 %copy-start.21 = (f32[768]{0:T(1024)S(1)}, f32[768]{0:T(1024)}, u32[]{:S(2)}) copy-start(f32[768]{0:T(1024)} %param.26) | copy-start | bytes 9220
  125.7 51.8 %copy-start.25 = (f32[768]{0:T(1024)S(1)}, f32[768]{0:T(1024)}, u32[]{:S(2)}) copy-start(f32[768]{0:T(1024)} %param.27) | copy-start | bytes 9220
  125.7 51.8 %copy-start.30 = (f32[768]{0:T(1024)S(1)}, f32[768]{0:T(1024)}, u32[]{:S(2)}) copy-start(f32[768]{0:T(1024)} %param.28) | copy-start | bytes 9220
  125.7 51.8 %copy-start.44 = (f32[3072]{0:T(1024)S(1)}, f32[3072]{0:T(1024)}, u32[]{:S(2)}) copy-start(f32[3072]{0:T(1024)} %param.30) | copy-start | bytes 36868
  125.7 147.4 %all-gather.5.cloned.1.call-start = ((), (), s32[]{:S(2)}) async-start(), calls=%async_computation.4 | async-start | bytes 5898240 | tf_op jit(solution)/shard_map/all_gather | solution.py:160
  173.7 3.8 copy-start.7
  175.5 71.2 %copy-start.23 = (f32[2,384]{1,0:T(2,128)}, f32[2,384]{1,0:T(2,128)S(1)}, u32[]{:S(2)}) copy-start(f32[2,384]{1,0:T(2,128)S(1)} %broadcast_multiply_fusion) | copy-start | bytes 9220
  177.5 69.2 %copy-start.27 = (f32[2,384]{1,0:T(2,128)}, f32[2,384]{1,0:T(2,128)S(1)}, u32[]{:S(2)}) copy-start(f32[2,384]{1,0:T(2,128)S(1)} %fusion.183) | copy-start | bytes 9220
  186.7 23.4 %copy-start.15 = (bf16[2,384,768]{2,1,0:T(8,128)(2,1)S(1)}, bf16[2,384,768]{2,1,0:T(8,128)(2,1)}, u32[]{:S(2)}) copy-start(bf16[2,384,768]{2,1,0:T(8,128)(2,1)} %param.33) | copy-start | bytes 3538948
  230.7 4.7 copy-start.9
  230.7 4.7 copy-start.34
  232.7 14.0 %copy-start.38 = (f32[2,384]{1,0:T(2,128)}, f32[2,384]{1,0:T(2,128)S(1)}, u32[]{:S(2)}) copy-start(f32[2,384]{1,0:T(2,128)S(1)} %negate_multiply_fusion.2) | copy-start | bytes 9220
  235.4 363.2 %all-reduce.11.cloned.1.call-start = ((), (), s32[]{:S(2)}) async-start(), calls=%async_computation.7 | async-start | bytes 37748736 | tf_op jit(solution)/shard_map/psum | solution.py:182
  255.7 17.3 %copy-start.29 = (bf16[192,768]{1,0:T(8,128)(2,1)S(1)}, bf16[192,768]{1,0:T(8,128)(2,1)}, u32[]{:S(2)}) copy-start(bf16[192,768]{1,0:T(8,128)(2,1)} %param.25) | copy-start | bytes 884740
  255.8 427.6 %all-reduce.13.cloned.1.call-start = ((), (), s32[]{:S(2)}) async-start(), calls=%async_computation.8 | async-start | bytes 2359296 | tf_op jit(solution)/shard_map/psum | solution.py:177
  278.3 2.8 copy-start.1
  281.3 4.9 copy-start.12
  285.2 3.7 copy-start.2
  291.4 7.6 copy-start.4
  293.8 4.2 copy-start.3
  391.5 14.2 %copy-start.13 = (bf16[3,64,512]{2,1,0:T(8,128)(2,1)S(1)}, bf16[3,64,512]{2,1,0:T(8,128)(2,1)}, u32[]{:S(2)}) copy-start(bf16[3,64,512]{2,1,0:T(8,128)(2,1)} %fusion.377) | copy-start | bytes 589828 | tf_op jit(solution)/shard_map/while
  391.5 14.2 %copy-start.14 = (bf16[3,64,512]{2,1,0:T(8,128)(2,1)S(1)}, bf16[3,64,512]{2,1,0:T(8,128)(2,1)}, u32[]{:S(2)}) copy-start(bf16[3,64,512]{2,1,0:T(8,128)(2,1)} %fusion.378) | copy-start | bytes 589828 | tf_op jit(solution)/shard_map/while
  407.1 2.9 copy-start.1
  410.2 4.9 copy-start.12
  414.1 3.7 copy-start.2
  420.3 7.7 copy-start.4
  422.7 4.3 copy-start.3
  520.4 14.3 %copy-start.13 = (bf16[3,64,512]{2,1,0:T(8,128)(2,1)S(1)}, bf16[3,64,512]{2,1,0:T(8,128)(2,1)}, u32[]{:S(2)}) copy-start(bf16[3,64,512]{2,1,0:T(8,128)(2,1)} %fusion.377) | copy-start | bytes 589828 | tf_op jit(solution)/shard_map/while
  520.4 14.3 %copy-start.14 = (bf16[3,64,512]{2,1,0:T(8,128)(2,1)S(1)}, bf16[3,64,512]{2,1,0:T(8,128)(2,1)}, u32[]{:S(2)}) copy-start(bf16[3,64,512]{2,1,0:T(8,128)(2,1)} %fusion.378) | copy-start | bytes 589828 | tf_op jit(solution)/shard_map/while
  545.3 4.7 copy-start.18
  556.3 176.8 %reduce-scatter.5.cloned.1.call-start = ((), (), s32[]{:S(2)}) async-start(), calls=%async_computation.5 | async-start | bytes 5898240 | tf_op jit(solution)/shard_map/reduce_scatter | solution.py:171
  564.0 743.3 %all-reduce.9.cloned.1.call-start = ((), (), s32[]{:S(2)}) async-start(), calls=%async_computation.6 | async-start | bytes 37748736 | tf_op jit(solution)/shard_map/psum | solution.py:181
  598.7 1.3 copy-start.6
  598.7 1.6 copy-start.8
  598.7 1.6 copy-start.22
  598.7 1.6 copy-start.48
  600.3 8.8 copy-start.19
  609.1 124.0 %copy-start.32 = (f32[2,384]{1,0:T(2,128)S(1)}, f32[2,384]{1,0:T(2,128)}, u32[]{:S(2)}) copy-start(f32[2,384]{1,0:T(2,128)} %copy-done.31) | copy-start | bytes 9220
  609.1 124.0 %copy-start.33 = (f32[768]{0:T(1024)S(1)}, f32[768]{0:T(1024)}, u32[]{:S(2)}) copy-start(f32[768]{0:T(1024)} %param.21) | copy-start | bytes 9220
  609.1 126.3 %copy-start.41 = (f32[2,384]{1,0:T(2,128)S(1)}, f32[2,384]{1,0:T(2,128)}, u32[]{:S(2)}) copy-start(f32[2,384]{1,0:T(2,128)} %copy-done.40) | copy-start | bytes 9220
  609.1 126.3 %copy-start.37 = (f32[2,384]{1,0:T(2,128)S(1)}, f32[2,384]{1,0:T(2,128)}, u32[]{:S(2)}) copy-start(f32[2,384]{1,0:T(2,128)} %copy-done.36) | copy-start | bytes 9220
  609.5 128.7 %copy-start.24 = (f32[2,384]{1,0:T(2,128)S(1)}, f32[2,384]{1,0:T(2,128)}, u32[]{:S(2)}) copy-start(f32[2,384]{1,0:T(2,128)} %copy-done.23) | copy-start | bytes 9220
  609.5 128.7 %copy-start.26 = (f32[768]{0:T(1024)S(1)}, f32[768]{0:T(1024)}, u32[]{:S(2)}) copy-start(f32[768]{0:T(1024)} %param.27) | copy-start | bytes 9220
  609.5 128.7 %copy-start.28 = (f32[2,384]{1,0:T(2,128)S(1)}, f32[2,384]{1,0:T(2,128)}, u32[]{:S(2)}) copy-start(f32[2,384]{1,0:T(2,128)} %copy-done.27) | copy-start | bytes 9220
  609.5 128.7 %copy-start.35 = (f32[2,384]{1,0:T(2,128)S(1)}, f32[2,384]{1,0:T(2,128)}, u32[]{:S(2)}) copy-start(f32[2,384]{1,0:T(2,128)} %copy-done.34) | copy-start | bytes 9220
  609.5 128.7 %copy-start.39 = (f32[2,384]{1,0:T(2,128)S(1)}, f32[2,384]{1,0:T(2,128)}, u32[]{:S(2)}) copy-start(f32[2,384]{1,0:T(2,128)} %copy-done.38) | copy-start | bytes 9220
  733.1 5.1 copy-start.10
  733.1 5.1 copy-start.11
  733.1 5.1 copy-start.16
  738.1 3.1 copy-start.42
  738.1 3.1 copy-start.43
  738.1 3.1 copy-start.45
  738.1 3.1 copy-start.46
  1307.4 8.8 slice-start
  1307.4 8.8 slice-start.1
  1307.4 8.8 slice-start.2
  (2 other events, 1.2 us)
Sparse Core Ops, SparseCore 0:
  14.7 40.1 all-gather.2
  125.8 47.8 reduce-scatter.2
  235.6 37.4 all-gather.4
  276.3 322.3 all-reduce.10
  602.6 80.7 all-reduce.12
  685.9 47.1 reduce-scatter.4
  737.4 569.9 all-reduce.8
